TPU v7x, 256 devices: a whole 4x4x8 slice. The times are simulated.
256 devices in a mesh: rows: 64 (over x, z, core), cols: 4 (over y).
Axes of the slice: x: 4, y: 4, z: 8, core: 2. Of those that a mesh axis runs over, the one named last changes fastest.
Arguments:
- block_list: int32 [512, 24], P('rows', 'cols'), may hold values from -1 to 511, as said below
- points: bfloat16 [16, 131072], P(None, 'rows'), may hold values from -4 to 4
- targets: float32 [32, 131072], P(None, 'rows'), may hold values from -6 to 6
Outputs:
- solution: float32 [32, 131072], P(None, 'rows')
- residual: float32 [32, 131072], P(None, 'rows')
Inputs may be any that keep to these rules, and one draw needn't show every extreme that they name: `block_list`: A non-empty entry j of block row i satisfies j <= i. Within the 6 slots of a block row held by one index of cols, the entries lie in different groups of 8 consecutive blocks. Of all slots held by one device (8 block rows of 6 slots), at most 1 name blocks of any one group of 8 consecutive blocks, and in every draw some device reaches 1.
All inputs are finite; a program needn't handle non-finite values.
Results may differ from a plain program's by a relative error of at most 0.0057.
Values may be sent and summed in bfloat16 or wider, within the bound.
A program may use at most 64 MiB of HBM per device.

v0:
```python
import jax
import jax.numpy as jnp
from jax import lax
from jax.sharding import PartitionSpec as P

ITERS = 2
REG = 1.5
RADIUS = 0.25


def wendland(left_x, right_x):
    left_f = left_x.astype(jnp.float32)
    right_f = right_x.astype(jnp.float32)
    left_sq = jnp.sum(left_f * left_f, axis=1)
    right_sq = jnp.sum(right_f * right_f, axis=1)
    inner_prod = jnp.einsum("nda,ndb->nab", left_f, right_f, precision=lax.Precision.HIGHEST)
    dist_sq = left_sq[:, :, None] + right_sq[:, None, :] - 2.0 * inner_prod
    scaled = jnp.sqrt(jnp.maximum(dist_sq, 0.0)) / RADIUS
    remain = jnp.maximum(1.0 - scaled, 0.0)
    square = remain * remain
    return square * square * (4.0 * scaled + 1.0)


def local(block_list, points, targets):
    row_count = lax.axis_size("rows")
    row_index = lax.axis_index("rows")
    block_rows, slot_width = block_list.shape
    coord_dim, npoints = points.shape
    outputs = targets.shape[0]
    block_len = npoints // block_rows
    slot_count = block_rows * slot_width
    capacity = (slot_count + row_count - 1) // row_count
    buffer_len = row_count * capacity
    turn_rows = 4
    turn_count = block_rows // turn_rows
    entries = block_list.reshape(slot_count)
    is_live = entries >= 0
    owners = jnp.where(is_live, entries // block_rows, 0)
    local_idx = jnp.where(is_live, entries - owners * block_rows, 0)
    first_row = row_index * block_rows
    row_global = first_row + jnp.arange(slot_count, dtype=jnp.int32) // slot_width
    off_diag = is_live & (entries != row_global)
    owner_hits = (
        (owners[:, None] == jnp.arange(row_count, dtype=jnp.int32)[None, :]) & is_live[:, None]
    ).astype(jnp.int32)
    slot_rank = jnp.sum((jnp.cumsum(owner_hits, axis=0) - owner_hits) * owner_hits, axis=1)
    place_at = jnp.where(is_live, owners * capacity + slot_rank, buffer_len)
    pick_at = jnp.minimum(place_at, buffer_len - 1)
    wanted = jnp.full((buffer_len,), -1, jnp.int32).at[place_at].set(local_idx, mode="drop")
    askers = jnp.full((buffer_len,), -1, jnp.int32).at[place_at].set(row_global, mode="drop")
    request = jnp.stack([wanted, askers], axis=1).reshape(row_count, capacity, 2)
    incoming = lax.all_to_all(request, "rows", split_axis=0, concat_axis=0, tiled=True).reshape(
        buffer_len, 2
    )
    in_live = incoming[:, 0] >= 0
    in_idx = jnp.maximum(incoming[:, 0], 0)
    collect_map = (
        (in_idx[None, :] == jnp.arange(block_rows, dtype=jnp.int32)[:, None]) & in_live[None, :]
    ).astype(jnp.float32)

    def serve(blocks):
        chosen = jnp.where(in_live[:, None, None], blocks[in_idx], jnp.zeros((), blocks.dtype))
        arrived = lax.all_to_all(
            chosen.reshape(row_count, capacity, blocks.shape[1], block_len),
            "rows",
            split_axis=0,
            concat_axis=0,
            tiled=True,
        )
        gotten = arrived.reshape(buffer_len, blocks.shape[1], block_len)[pick_at]
        return jnp.where(is_live[:, None, None], gotten, jnp.zeros((), gotten.dtype))

    def collect(terms):
        flat = terms.reshape(buffer_len, -1)
        summed = jnp.dot(
            collect_map, flat, precision=lax.Precision.HIGHEST, preferred_element_type=jnp.float32
        )
        return summed.reshape(block_rows, terms.shape[1], block_len)

    def give_back(mirror):
        placed = (
            jnp.zeros((buffer_len,) + mirror.shape[1:], jnp.float32)
            .at[place_at]
            .set(mirror, mode="drop")
        )
        arrived = lax.all_to_all(
            placed.reshape(row_count, capacity, mirror.shape[1], block_len),
            "rows",
            split_axis=0,
            concat_axis=0,
            tiled=True,
        )
        return collect(arrived.reshape(buffer_len, mirror.shape[1], block_len))

    def column_total(partial_value):
        return lax.psum(partial_value, "cols")

    def global_sum(values):
        return lax.psum(values, "rows")

    own_x = points.reshape(coord_dim, block_rows, block_len).transpose(1, 0, 2)
    far_x = serve(own_x)
    grouped_x = own_x.reshape(turn_count, turn_rows, coord_dim, block_len)
    grouped_far = far_x.reshape(turn_count, turn_rows * slot_width, coord_dim, block_len)
    grouped_live = is_live.reshape(turn_count, turn_rows * slot_width)
    grouped_off = off_diag.reshape(turn_count, turn_rows * slot_width)

    def row_pass(own_w, far_w):

        def row_step(pieces):
            near_x, remote_x, live_now, off_now = (pieces[0], pieces[1], pieces[2], pieces[3])
            values = jnp.where(
                live_now[:, None, None],
                wendland(jnp.repeat(near_x, slot_width, axis=0), remote_x),
                0.0,
            )
            if own_w is None:
                direct = jnp.sum(
                    jnp.sum(values, axis=2).reshape(turn_rows, slot_width, block_len), axis=1
                )[:, None, :]
                mirror = jnp.where(off_now[:, None], jnp.sum(values, axis=1), 0.0)[:, None, :]
                return (direct, mirror)
            kernel_bf = values.astype(jnp.bfloat16)
            direct = jnp.einsum(
                "nab,nob->noa", kernel_bf, pieces[5], preferred_element_type=jnp.float32
            )
            direct = jnp.sum(direct.reshape(turn_rows, slot_width, outputs, block_len), axis=1)
            mirror = jnp.einsum(
                "nab,noa->nob",
                kernel_bf,
                jnp.repeat(pieces[4], slot_width, axis=0),
                preferred_element_type=jnp.float32,
            )
            return (direct, jnp.where(off_now[:, None, None], mirror, 0.0))

        pieces = (grouped_x, grouped_far, grouped_live, grouped_off)
        if own_w is not None:
            pieces = pieces + (
                own_w.reshape(turn_count, turn_rows, outputs, block_len),
                far_w.reshape(turn_count, turn_rows * slot_width, outputs, block_len),
            )
        results = lax.map(row_step, pieces)
        channels = results[0].shape[2]
        direct = results[0].reshape(block_rows, channels, block_len)
        return (direct, results[1].reshape(slot_count, channels, block_len))

    direct, mirror = row_pass(None, None)
    degree_part = direct + give_back(mirror)
    inv_root = 1.0 / jnp.sqrt(1.0 + column_total(degree_part))
    resid = targets.reshape(outputs, block_rows, block_len).transpose(1, 0, 2)
    direction = resid
    solution = jnp.zeros_like(resid)
    norm_now = global_sum(jnp.sum(resid * resid, axis=(0, 2)))
    for iteration in range(ITERS):
        weights = (direction * inv_root).astype(jnp.bfloat16)
        apply_far_w = serve(weights)
        apply_direct, apply_mirror = row_pass(weights, apply_far_w)
        apply_partial_value = apply_direct + give_back(apply_mirror)
        applied = REG * direction + inv_root * column_total(apply_partial_value)
        step_size = norm_now / global_sum(jnp.sum(direction * applied, axis=(0, 2)))
        solution = solution + step_size[None, :, None] * direction
        resid = resid - step_size[None, :, None] * applied
        if iteration + 1 < ITERS:
            norm_next = global_sum(jnp.sum(resid * resid, axis=(0, 2)))
            direction = resid + (norm_next / norm_now)[None, :, None] * direction
            norm_now = norm_next
    return (
        solution.transpose(1, 0, 2).reshape(outputs, npoints),
        resid.transpose(1, 0, 2).reshape(outputs, npoints),
    )


def solution(mesh):
    placed = (P("rows", "cols"), P(None, "rows"), P(None, "rows"))
    return jax.shard_map(
        local,
        mesh=mesh,
        in_specs=placed,
        out_specs=(P(None, "rows"), P(None, "rows")),
        check_vma=False,
    )
```

profile of v0, /device:TPU:16, one launch (start us, length us, event | category | flops | bytes accessed | tf_op | source)
XLA Modules:
  0.0 810.2 jit_solution(6442422851500337374)
XLA Ops:
  11.4 11.9 %all-to-all-start = ((s32[64,1,2]{2,1,0:T(1,128)}), s32[64,1,2]{2,1,0:T(1,128)S(1)}, u32[]{:S(2)}, u32[]{:S(2)}) async-start(s32[64,1,2]{2,1,0:T(1,128)} %copy.22), calls=%async_computation | async-start | bytes 65536 | tf_op jit(solution)/shard_map/all_to_all | solution.py:52
  24.2 8.6 %all-to-all-done = s32[64,1,2]{2,1,0:T(1,128)S(1)} async-done(((s32[64,1,2]{2,1,0:T(1,128)}), s32[64,1,2]{2,1,0:T(1,128)S(1)}, u32[]{:S(2)}, u32[]{:S(2)}) %all-to-all-start) | async-done | bytes 544 | tf_op jit(solution)/shard_map/all_to_all | solution.py:52
  39.1 17.1 %all-to-all-done.1 = bf16[64,1,16,256]{3,2,1,0:T(8,128)(2,1)S(1)} async-done(((bf16[64,1,16,256]{3,2,1,0:T(8,128)(2,1)}), bf16[64,1,16,256]{3,2,1,0:T(8,128)(2,1)S(1)}, u32[]{:S(2)}, u32[]{:S(2)}) %all-to-all-start.1) | async-done | bytes 524320 | tf_op jit(solution)/shard_map/all_to_all | solution.py:63
  56.9 12.5 %while.42 = (s32[]{:T(128)}, f32[2,4,1,256]{3,2,1,0:T(1,128)S(1)}, f32[2,24,1,256]{3,1,2,0:T(8,128)S(1)}, pred[2,24]{1,0:T(4,128)(4,1)S(1)}, bf16[2,4,16,256]{3,...) while((s32[]{:T(128)}, f32[2,4,1,256]{3,2,1,0:T(1,128)S(1)}, ...), condition=%wide.region_12.13_spmd, body=%wide.region_6.12_spmd.sunk | while | flops 74260480 | bytes 1274609 | solution.py:142
  57.2 5.8 fusion.105
  63.4 5.9 fusion.105
  70.9 6.4 all-to-all-start.2
  77.5 9.6 %all-to-all-done.2 = f32[64,1,1,256]{3,2,1,0:T(1,128)S(1)} async-done(((f32[64,1,1,256]{3,2,1,0:T(1,128)}), f32[64,1,1,256]{3,2,1,0:T(1,128)S(1)}, u32[]{:S(2)}, u32[]{:S(2)}) %all-to-all-start.2) | async-done | bytes 65568 | tf_op jit(solution)/shard_map/all_to_all | solution.py:86
  87.2 8.5 %psum.50 = f32[8,1,256]{2,0,1:T(8,128)S(1)} all-reduce(f32[8,1,256]{2,0,1:T(8,128)S(1)} %fusion.37), channel_id=1, replica_groups=mesh['rows'=64,'cols'=4] {'cols'}, use_global_device_ids=true, to_apply=%region_14.15 | all-reduce | flops 2048 | bytes 16384 | tf_op jit(solution)/shard_map/psum | solution.py:96
  102.3 28.1 %all-to-all-done.3 = bf16[64,1,32,256]{3,2,1,0:T(8,128)(2,1)S(1)} async-done(((bf16[64,1,32,256]{3,2,1,0:T(8,128)(2,1)}), bf16[64,1,32,256]{3,2,1,0:T(8,128)(2,1)S(1)}, u32[]{:S(2)}, u32[]{:S(2)}) %all-to-all-start.3) | async-done | bytes 1048608 | tf_op jit(solution)/shard_map/all_to_all | solution.py:63
  132.5 16.1 %while.43 = (s32[]{:T(128)}, f32[2,4,32,256]{3,2,1,0:T(8,128)S(1)}, f32[2,24,32,256]{3,2,1,0:T(8,128)}, bf16[2,24,32,256]{3,2,1,0:T(8,128)(2,1)S(1)}, pred[2,24]...) while((s32[]{:T(128)}, f32[2,4,32,256]{3,2,1,0:T(8,128)S(1)}, ...), condition=%wide.region_19.20_spmd, body=%wide.region_15.19_spmd.sunk | while | flops 274375680 | bytes 14607621 | solution.py:142
  132.7 5.1 select_convert_fusion.4
  148.9 5.1 scatter_fusion
  154.1 57.7 %all_to_all.35 = f32[64,1,32,256]{3,2,1,0:T(8,128)S(1)} all-to-all(f32[64,1,32,256]{3,2,1,0:T(8,128)S(1)} %bitcast.324), channel_id=1, replica_groups=mesh['rows'=64,'cols'=4] {'rows'}, dimensions={0} | all-to-all | bytes 4194304 | tf_op jit(solution)/shard_map/all_to_all | solution.py:86
  214.5 42.9 %all-reduce.4.cloned.1.call-done = f32[8,32,256]{2,0,1:T(8,128)} async-done(((f32[8,32,256]{2,0,1:T(8,128)}), f32[8,32,256]{2,0,1:T(8,128)}) %all-reduce.4.cloned.1.call-update) | async-done | bytes 262160 | tf_op jit(solution)/shard_map/psum | solution.py:96
  258.6 127.0 %all-reduce = (f32[32]{0:T(128)S(1)}, f32[32]{0:T(128)S(1)}) all-reduce(f32[32]{0:T(128)S(1)} %get-tuple-element.383, f32[32]{0:T(128)S(1)} %get-tuple-element.382), channel_id=1, replica_groups=mesh['rows'=64,'cols'=4] {'rows'}, use_global_device_ids=true, to_apply=%region_1.2 | all-reduce | flops 64 | bytes 512 | tf_op jit(solution)/shard_map/psum | solution.py:99
  387.1 124.0 %psum.53 = f32[32]{0:T(128)S(1)} all-reduce(f32[32]{0:T(128)S(1)} %multiply_reduce_fusion.7), channel_id=1, replica_groups=mesh['rows'=64,'cols'=4] {'rows'}, use_global_device_ids=true, to_apply=%region_25.26 | all-reduce | flops 32 | bytes 256 | tf_op jit(solution)/shard_map/psum | solution.py:99
  513.1 32.0 %all_to_all.37 = bf16[64,1,32,256]{3,2,1,0:T(8,128)(2,1)S(1)} all-to-all(bf16[64,1,32,256]{3,2,1,0:T(8,128)(2,1)S(1)} %fusion.38), channel_id=1, replica_groups=mesh['rows'=64,'cols'=4] {'rows'}, dimensions={0} | all-to-all | bytes 2097152 | tf_op jit(solution)/shard_map/all_to_all | solution.py:63
  547.2 16.1 %while.44 = (s32[]{:T(128)}, f32[2,4,32,256]{3,2,1,0:T(8,128)S(1)}, f32[2,24,32,256]{3,2,1,0:T(8,128)}, bf16[2,24,32,256]{3,2,1,0:T(8,128)(2,1)S(1)}, pred[2,24]...) while((s32[]{:T(128)}, f32[2,4,32,256]{3,2,1,0:T(8,128)S(1)}, ...), condition=%wide.region_30.31_spmd, body=%wide.region_26.30_spmd.sunk | while | flops 274375680 | bytes 14607621 | solution.py:142
  547.4 5.1 select_convert_fusion.5
  563.6 5.1 scatter_fusion.1
  568.8 57.7 %all_to_all.36 = f32[64,1,32,256]{3,2,1,0:T(8,128)S(1)} all-to-all(f32[64,1,32,256]{3,2,1,0:T(8,128)S(1)} %bitcast.323), channel_id=1, replica_groups=mesh['rows'=64,'cols'=4] {'rows'}, dimensions={0} | all-to-all | bytes 4194304 | tf_op jit(solution)/shard_map/all_to_all | solution.py:86
  629.2 42.9 %all-reduce.6.cloned.1.call-done = f32[8,32,256]{2,0,1:T(8,128)} async-done(((f32[8,32,256]{2,0,1:T(8,128)}), f32[8,32,256]{2,0,1:T(8,128)}) %all-reduce.6.cloned.1.call-update) | async-done | bytes 262160 | tf_op jit(solution)/shard_map/psum | solution.py:96
  673.6 127.0 %psum.55 = f32[32]{0:T(128)S(1)} all-reduce(f32[32]{0:T(128)S(1)} %multiply_reduce_fusion.6), channel_id=1, replica_groups=mesh['rows'=64,'cols'=4] {'rows'}, use_global_device_ids=true, to_apply=%region_34.35 | all-reduce | flops 32 | bytes 256 | tf_op jit(solution)/shard_map/psum | solution.py:99
  (154 shorter events, 61.5 us)
Async XLA Ops:
  7.2 31.9 %copy-start.5 = (s32[8,6]{1,0:T(8,128)S(1)}, s32[8,6]{1,0:T(8,128)}, u32[]{:S(2)}) copy-start(s32[8,6]{1,0:T(8,128)} %param.9) | copy-start | bytes 580
  11.4 21.4 %all-to-all-start = ((s32[64,1,2]{2,1,0:T(1,128)}), s32[64,1,2]{2,1,0:T(1,128)S(1)}, u32[]{:S(2)}, u32[]{:S(2)}) async-start(s32[64,1,2]{2,1,0:T(1,128)} %copy.22), calls=%async_computation | async-start | bytes 65536 | tf_op jit(solution)/shard_map/all_to_all | solution.py:52
  34.4 21.8 %all-to-all-start.1 = ((bf16[64,1,16,256]{3,2,1,0:T(8,128)(2,1)}), bf16[64,1,16,256]{3,2,1,0:T(8,128)(2,1)S(1)}, u32[]{:S(2)}, u32[]{:S(2)}) async-start(bf16[64,1,16,256]{3,2,1,0:T(8,128)(2,1)} %bitcast_select_fusion.2), calls=%async_computation.1 | async-start | bytes 1048576 | tf_op jit(solution)/shard_map/all_to_all | solution.py:63
  56.9 20.4 %copy-start.4 = (f32[32,2048]{1,0:T(8,128)S(1)}, f32[32,2048]{1,0:T(8,128)}, u32[]{:S(2)}) copy-start(f32[32,2048]{1,0:T(8,128)} %param.11) | copy-start | bytes 786436
  70.9 16.2 %all-to-all-start.2 = ((f32[64,1,1,256]{3,2,1,0:T(1,128)}), f32[64,1,1,256]{3,2,1,0:T(1,128)S(1)}, u32[]{:S(2)}, u32[]{:S(2)}) async-start(f32[64,1,1,256]{3,2,1,0:T(1,128)} %reshape.420), calls=%async_computation.2 | async-start | bytes 131072 | tf_op jit(solution)/shard_map/all_to_all | solution.py:86
  77.4 20.1 %copy-start = (f32[4,8,8,256]{3,2,1,0:T(8,128)}, f32[4,8,8,256]{3,2,1,0:T(8,128)S(1)}, u32[]{:S(2)}) copy-start(f32[4,8,8,256]{3,2,1,0:T(8,128)S(1)} %copy.51) | copy-start | bytes 786436
  97.5 32.8 %all-to-all-start.3 = ((bf16[64,1,32,256]{3,2,1,0:T(8,128)(2,1)}), bf16[64,1,32,256]{3,2,1,0:T(8,128)(2,1)S(1)}, u32[]{:S(2)}, u32[]{:S(2)}) async-start(bf16[64,1,32,256]{3,2,1,0:T(8,128)(2,1)} %fusion.39), calls=%async_computation.3 | async-start | bytes 2097152 | tf_op jit(solution)/shard_map/all_to_all | solution.py:63
  102.2 155.1 %all-reduce.4.cloned.1.call-start = ((), (), s32[]{:S(2)}) async-start(), calls=%async_computation.7 | async-start | bytes 524288 | tf_op jit(solution)/shard_map/psum | solution.py:96
  154.1 103.3 %copy-start.1 = (f32[4,8,8,256]{3,2,1,0:T(8,128)S(1)}, f32[4,8,8,256]{3,2,1,0:T(8,128)}, u32[]{:S(2)}) copy-start(f32[4,8,8,256]{3,2,1,0:T(8,128)} %copy-done) | copy-start | bytes 786436
  214.4 457.6 %all-reduce.6.cloned.1.call-start = ((), (), s32[]{:S(2)}) async-start(), calls=%async_computation.8 | async-start | bytes 524288 | tf_op jit(solution)/shard_map/psum | solution.py:96
  568.8 103.3 %copy-start.2 = (f32[4,8,8,256]{3,2,1,0:T(8,128)S(1)}, f32[4,8,8,256]{3,2,1,0:T(8,128)}, u32[]{:S(2)}) copy-start(f32[4,8,8,256]{3,2,1,0:T(8,128)} %copy-done) | copy-start | bytes 786436
  568.8 103.3 %copy-start.3 = (f32[8,32,256]{2,0,1:T(8,128)S(1)}, f32[8,32,256]{2,0,1:T(8,128)}, u32[]{:S(2)}) copy-start(f32[8,32,256]{2,0,1:T(8,128)} %all-reduce.4.cloned.1.call-done) | copy-start | bytes 786436
Sparse Core Ops, SparseCore 0:
  214.5 42.7 all-reduce.3
  629.3 42.7 all-reduce.5
where the time goes:
time: 811 us; the launch traced here: 810 us
  blocking collectives  534 us (66%)
  waiting for transfers between devices  149 us (18%)
  matrix products  47.9 us (6%)
  starting transfers between devices  27.7 us (3%)
  local copies, waits for them, and re-layouts  25.6 us (3%)
  between operations  14.4 us (2%)
  other arithmetic  10.8 us (1%)
    psum x3, blocking collectives, global_sum(): return lax.psum(values, 'rows')  378 us
    all_to_all x2, blocking collectives, give_back(): lax.all_to_all(placed.reshape(row_count, capacity, mirror.shape[1], block...  115 us
    psum x2, waiting for transfers between devices, column_total(): return lax.psum(partial_value, 'cols')  85.8 us
    all_to_all x2, waiting for transfers between devices, serve(): lax.all_to_all(chosen.reshape(row_count, capacity, blocks.shape[1], block...  45.2 us
    dot_general x6, matrix products, wendland(): jnp.einsum('nda,ndb->nab', left_f, right_f, precision=lax.Precision.HIGHEST)  32.3 us
    all_to_all x1, blocking collectives, serve(): lax.all_to_all(chosen.reshape(row_count, capacity, blocks.shape[1], block...  32 us
  transfers between devices with their start and end apart: 6, of which 6 were waited for; matrix products, arithmetic and copies ran while one was open for 0% of the time, Pallas kernels for 0%

commit v1 on v0

--- a/solution.py
+++ b/solution.py
@@ -6,6 +6,11 @@
 ITERS = 2
 REG = 1.5
 RADIUS = 0.25
+
+
+def summed_here(x, axis):
+    shards = lax.all_gather(x, axis)
+    return jnp.sum(shards, axis=0)
 
 
 def wendland(left_x, right_x):
@@ -96,7 +101,7 @@
         return lax.psum(partial_value, "cols")
 
     def global_sum(values):
-        return lax.psum(values, "rows")
+        return summed_here(values, "rows")
 
     own_x = points.reshape(coord_dim, block_rows, block_len).transpose(1, 0, 2)
     far_x = serve(own_x)

time: 811 us -> 939 us (1.16)
  blocking collectives: 534 us -> 660 us
    unnamed x0 -> x3, blocking collectives: none -> 504 us
    psum x3 -> x0, blocking collectives: 378 us -> none  [global_sum(): return lax.psum(values, 'rows')]
where the time goes in v1:
time: 939 us; the launch traced here: 938 us
  blocking collectives  660 us (70%)
  waiting for transfers between devices  148 us (16%)
  matrix products  48 us (5%)
  local copies, waits for them, and re-layouts  27.7 us (3%)
  starting transfers between devices  27.7 us (3%)
  between operations  15.2 us (2%)
  other arithmetic  10.9 us (1%)
    unnamed x3, blocking collectives  504 us
    all_to_all x2, blocking collectives, give_back(): lax.all_to_all(placed.reshape(row_count, capacity, mirror.shape[1], block...  115 us
    psum x2, waiting for transfers between devices, column_total(): return lax.psum(partial_value, 'cols')  84.4 us
    all_to_all x2, waiting for transfers between devices, serve(): lax.all_to_all(chosen.reshape(row_count, capacity, blocks.shape[1], block...  45.2 us
    dot_general x6, matrix products, wendland(): jnp.einsum('nda,ndb->nab', left_f, right_f, precision=lax.Precision.HIGHEST)  32.3 us
    all_to_all x1, blocking collectives, serve(): lax.all_to_all(chosen.reshape(row_count, capacity, blocks.shape[1], block...  32 us
  transfers between devices with their start and end apart: 6, of which 6 were waited for; matrix products, arithmetic and copies ran while one was open for 0% of the time, Pallas kernels for 0%

profile of v1, /device:TPU:16, one launch (start us, length us, event | category | flops | bytes accessed | tf_op | source)
XLA Modules:
  0.0 937.7 jit_solution(7840834377341587639)
XLA Ops:
  11.4 11.9 %all-to-all-start = ((s32[64,1,2]{2,1,0:T(1,128)}), s32[64,1,2]{2,1,0:T(1,128)S(1)}, u32[]{:S(2)}, u32[]{:S(2)}) async-start(s32[64,1,2]{2,1,0:T(1,128)} %copy.22), calls=%async_computation | async-start | bytes 65536 | tf_op jit(solution)/shard_map/all_to_all | solution.py:57
  24.2 8.6 all-to-all-done
  39.1 17.1 %all-to-all-done.1 = bf16[64,1,16,256]{3,2,1,0:T(8,128)(2,1)S(1)} async-done(((bf16[64,1,16,256]{3,2,1,0:T(8,128)(2,1)}), bf16[64,1,16,256]{3,2,1,0:T(8,128)(2,1)S(1)}, u32[]{:S(2)}, u32[]{:S(2)}) %all-to-all-start.1) | async-done | bytes 524320 | tf_op jit(solution)/shard_map/all_to_all | solution.py:68
  56.9 12.5 %while.42 = (s32[]{:T(128)}, f32[2,4,1,256]{3,2,1,0:T(1,128)S(1)}, f32[2,24,1,256]{3,1,2,0:T(8,128)S(1)}, pred[2,24]{1,0:T(4,128)(4,1)S(1)}, bf16[2,4,16,256]{3,...) while((s32[]{:T(128)}, f32[2,4,1,256]{3,2,1,0:T(1,128)S(1)}, ...), condition=%wide.region_12.13_spmd, body=%wide.region_6.12_spmd.sunk | while | flops 74260480 | bytes 1274609 | solution.py:147
  57.2 5.9 fusion.105
  63.4 5.9 fusion.105
  70.9 6.4 all-to-all-start.2
  77.5 9.6 %all-to-all-done.2 = f32[64,1,1,256]{3,2,1,0:T(1,128)S(1)} async-done(((f32[64,1,1,256]{3,2,1,0:T(1,128)}), f32[64,1,1,256]{3,2,1,0:T(1,128)S(1)}, u32[]{:S(2)}, u32[]{:S(2)}) %all-to-all-start.2) | async-done | bytes 65568 | tf_op jit(solution)/shard_map/all_to_all | solution.py:91
  87.2 8.5 psum.21
  102.2 28.1 %all-to-all-done.3 = bf16[64,1,32,256]{3,2,1,0:T(8,128)(2,1)S(1)} async-done(((bf16[64,1,32,256]{3,2,1,0:T(8,128)(2,1)}), bf16[64,1,32,256]{3,2,1,0:T(8,128)(2,1)S(1)}, u32[]{:S(2)}, u32[]{:S(2)}) %all-to-all-start.3) | async-done | bytes 1048608 | tf_op jit(solution)/shard_map/all_to_all | solution.py:68
  132.5 16.1 %while.43 = (s32[]{:T(128)}, f32[2,4,32,256]{3,2,1,0:T(8,128)S(1)}, f32[2,24,32,256]{3,2,1,0:T(8,128)}, bf16[2,24,32,256]{3,2,1,0:T(8,128)(2,1)S(1)}, pred[2,24]...) while((s32[]{:T(128)}, f32[2,4,32,256]{3,2,1,0:T(8,128)S(1)}, ...), condition=%wide.region_19.20_spmd, body=%wide.region_15.19_spmd.sunk | while | flops 274375680 | bytes 14607621 | solution.py:147
  132.7 5.1 select_convert_fusion.4
  148.9 5.1 scatter_fusion
  154.1 57.7 %all_to_all.35 = f32[64,1,32,256]{3,2,1,0:T(8,128)S(1)} all-to-all(f32[64,1,32,256]{3,2,1,0:T(8,128)S(1)} %bitcast.325), channel_id=1, replica_groups=mesh['rows'=64,'cols'=4] {'rows'}, dimensions={0} | all-to-all | bytes 4194304 | tf_op jit(solution)/shard_map/all_to_all | solution.py:91
  215.8 41.5 %all-reduce.8.cloned.1.call-done = f32[8,32,256]{2,0,1:T(8,128)} async-done(((f32[8,32,256]{2,0,1:T(8,128)}), f32[8,32,256]{2,0,1:T(8,128)}) %all-reduce.8.cloned.1.call-update) | async-done | bytes 262160 | tf_op jit(solution)/shard_map/psum | solution.py:101
  259.2 249.0 %all-reduce.4 = (f32[2048]{0:T(1024)S(1)}, f32[2048]{0:T(1024)S(1)}) all-reduce(f32[2048]{0:T(1024)S(1)} %dynamic-update-slice, f32[2048]{0:T(1024)S(1)} %dynamic-update-slice.1), channel_id=2, replica_groups=mesh['rows'=64,'cols'=4] {'rows'}, use_global_device_ids=true, to_apply=%add | all-reduce | flops 4096 | bytes 32768
  510.1 126.1 %all-reduce.2 = f32[2048]{0:T(1024)S(1)} all-reduce(f32[2048]{0:T(1024)S(1)} %dynamic-update-slice.2), channel_id=4, replica_groups=mesh['rows'=64,'cols'=4] {'rows'}, use_global_device_ids=true, to_apply=%add.2 | all-reduce | flops 2048 | bytes 16384
  638.2 32.0 %all_to_all.37 = bf16[64,1,32,256]{3,2,1,0:T(8,128)(2,1)S(1)} all-to-all(bf16[64,1,32,256]{3,2,1,0:T(8,128)(2,1)S(1)} %fusion.38), channel_id=1, replica_groups=mesh['rows'=64,'cols'=4] {'rows'}, dimensions={0} | all-to-all | bytes 2097152 | tf_op jit(solution)/shard_map/all_to_all | solution.py:68
  672.4 16.1 %while.44 = (s32[]{:T(128)}, f32[2,4,32,256]{3,2,1,0:T(8,128)S(1)}, f32[2,24,32,256]{3,2,1,0:T(8,128)}, bf16[2,24,32,256]{3,2,1,0:T(8,128)(2,1)S(1)}, pred[2,24]...) while((s32[]{:T(128)}, f32[2,4,32,256]{3,2,1,0:T(8,128)S(1)}, ...), condition=%wide.region_30.31_spmd, body=%wide.region_26.30_spmd.sunk | while | flops 274375680 | bytes 14607621 | solution.py:147
  672.6 5.1 select_convert_fusion.5
  688.8 5.1 scatter_fusion.1
  693.9 57.7 %all_to_all.36 = f32[64,1,32,256]{3,2,1,0:T(8,128)S(1)} all-to-all(f32[64,1,32,256]{3,2,1,0:T(8,128)S(1)} %bitcast.324), channel_id=1, replica_groups=mesh['rows'=64,'cols'=4] {'rows'}, dimensions={0} | all-to-all | bytes 4194304 | tf_op jit(solution)/shard_map/all_to_all | solution.py:91
  754.3 42.9 %all-reduce.10.cloned.1.call-done = f32[8,32,256]{2,0,1:T(8,128)} async-done(((f32[8,32,256]{2,0,1:T(8,128)}), f32[8,32,256]{2,0,1:T(8,128)}) %all-reduce.10.cloned.1.call-update) | async-done | bytes 262160 | tf_op jit(solution)/shard_map/psum | solution.py:101
  799.0 129.0 %all-reduce.3 = f32[2048]{0:T(1024)S(1)} all-reduce(f32[2048]{0:T(1024)S(1)} %dynamic-update-slice.3), channel_id=5, replica_groups=mesh['rows'=64,'cols'=4] {'rows'}, use_global_device_ids=true, to_apply=%add.3 | all-reduce | flops 2048 | bytes 16384
  (173 shorter events, 63.6 us)
Async XLA Ops:
  7.2 31.9 %copy-start.5 = (s32[8,6]{1,0:T(8,128)S(1)}, s32[8,6]{1,0:T(8,128)}, u32[]{:S(2)}) copy-start(s32[8,6]{1,0:T(8,128)} %param.9) | copy-start | bytes 580
  11.4 21.4 %all-to-all-start = ((s32[64,1,2]{2,1,0:T(1,128)}), s32[64,1,2]{2,1,0:T(1,128)S(1)}, u32[]{:S(2)}, u32[]{:S(2)}) async-start(s32[64,1,2]{2,1,0:T(1,128)} %copy.22), calls=%async_computation | async-start | bytes 65536 | tf_op jit(solution)/shard_map/all_to_all | solution.py:57
  34.4 21.8 %all-to-all-start.1 = ((bf16[64,1,16,256]{3,2,1,0:T(8,128)(2,1)}), bf16[64,1,16,256]{3,2,1,0:T(8,128)(2,1)S(1)}, u32[]{:S(2)}, u32[]{:S(2)}) async-start(bf16[64,1,16,256]{3,2,1,0:T(8,128)(2,1)} %bitcast_select_fusion.2), calls=%async_computation.1 | async-start | bytes 1048576 | tf_op jit(solution)/shard_map/all_to_all | solution.py:68
  56.9 20.4 %copy-start.4 = (f32[32,2048]{1,0:T(8,128)S(1)}, f32[32,2048]{1,0:T(8,128)}, u32[]{:S(2)}) copy-start(f32[32,2048]{1,0:T(8,128)} %param.11) | copy-start | bytes 786436
  70.9 16.1 %all-to-all-start.2 = ((f32[64,1,1,256]{3,2,1,0:T(1,128)}), f32[64,1,1,256]{3,2,1,0:T(1,128)S(1)}, u32[]{:S(2)}, u32[]{:S(2)}) async-start(f32[64,1,1,256]{3,2,1,0:T(1,128)} %reshape.432), calls=%async_computation.2 | async-start | bytes 131072 | tf_op jit(solution)/shard_map/all_to_all | solution.py:91
  77.4 20.1 %copy-start = (f32[4,8,8,256]{3,2,1,0:T(8,128)}, f32[4,8,8,256]{3,2,1,0:T(8,128)S(1)}, u32[]{:S(2)}) copy-start(f32[4,8,8,256]{3,2,1,0:T(8,128)S(1)} %copy.55) | copy-start | bytes 786436
  97.5 32.8 %all-to-all-start.3 = ((bf16[64,1,32,256]{3,2,1,0:T(8,128)(2,1)}), bf16[64,1,32,256]{3,2,1,0:T(8,128)(2,1)S(1)}, u32[]{:S(2)}, u32[]{:S(2)}) async-start(bf16[64,1,32,256]{3,2,1,0:T(8,128)(2,1)} %fusion.39), calls=%async_computation.3 | async-start | bytes 2097152 | tf_op jit(solution)/shard_map/all_to_all | solution.py:68
  102.2 155.1 %all-reduce.8.cloned.1.call-start = ((), (), s32[]{:S(2)}) async-start(), calls=%async_computation.7 | async-start | bytes 524288 | tf_op jit(solution)/shard_map/psum | solution.py:101
  154.0 60.4 %copy-start.6 = (u32[256]{0:T(256)S(1)}, u32[256]{0:T(256)}, u32[]{:S(2)}) copy-start(u32[256]{0:T(256)} %constant.223) | copy-start | bytes 3076
  154.0 103.3 %copy-start.1 = (f32[4,8,8,256]{3,2,1,0:T(8,128)S(1)}, f32[4,8,8,256]{3,2,1,0:T(8,128)}, u32[]{:S(2)}) copy-start(f32[4,8,8,256]{3,2,1,0:T(8,128)} %copy-done) | copy-start | bytes 786436
  214.4 582.8 %all-reduce.10.cloned.1.call-start = ((), (), s32[]{:S(2)}) async-start(), calls=%async_computation.8 | async-start | bytes 524288 | tf_op jit(solution)/shard_map/psum | solution.py:101
  693.9 103.3 %copy-start.2 = (f32[4,8,8,256]{3,2,1,0:T(8,128)S(1)}, f32[4,8,8,256]{3,2,1,0:T(8,128)}, u32[]{:S(2)}) copy-start(f32[4,8,8,256]{3,2,1,0:T(8,128)} %copy-done) | copy-start | bytes 786436
  693.9 103.3 %copy-start.3 = (f32[8,32,256]{2,0,1:T(8,128)S(1)}, f32[8,32,256]{2,0,1:T(8,128)}, u32[]{:S(2)}) copy-start(f32[8,32,256]{2,0,1:T(8,128)} %all-reduce.8.cloned.1.call-done) | copy-start | bytes 786436
Sparse Core Ops, SparseCore 0:
  214.5 42.7 all-reduce.7
  754.4 42.7 all-reduce.9
